TPU v7x, 512 devices: a whole 4x4x16 slice. The times are simulated.
512 devices in a mesh: seq: 64 (over z, y), head: 8 (over x, core).
Axes of the slice: x: 4, y: 4, z: 16, core: 2. Of those that a mesh axis runs over, the one named last changes fastest.
Arguments:
- stream_x: bfloat16 [16384, 3072], P('seq', 'head')
- qkv_weight: bfloat16 [3072, 4608], P(None, 'head')
- short_lengths: int32 [32], replicated, may hold values from 1 to 256, 4096 in all
- cache_owner: int32 [16384, 1], P('seq'), may hold values from 0 to 63, as said below
Outputs:
- attended: bfloat16 [16384, 1536], P('seq', 'head')
- row_lse: float32 [16, 16384], P('head', 'seq')
- kv_cache: bfloat16 [32768, 3072], P('seq', 'head')
Inputs may be any that keep to these rules, and one draw needn't show every extreme that they name: `short_lengths`: the lengths sum to 4096 and the longest is exactly 256. `cache_owner`: the rows of one device form 256 / 8 aligned pages of 8 rows; all rows of a page name the same owner, and the pages of one device name different owners, so an owner takes either none or exactly 8 rows of one device.
All inputs are finite; a program needn't handle non-finite values.
Results may differ from a plain program's by a relative error of at most 0.0083.
Values may be sent and summed in bfloat16 or wider, within the bound.
No kernel may reach another device: no remote copies, remote signals or barrier semaphores. Data moves between devices by JAX's collectives and lax.ppermute only.
A program may use at most 128 MiB of HBM per device.

v0:
```python
import math

import jax
import jax.numpy as jnp
from jax import lax
from jax.sharding import PartitionSpec as P

HD = 96


neg_large = -1e30
rope_base = 10000.0


def boundaries(short_lengths, long_length):
    running = jnp.cumsum(short_lengths)
    return jnp.concatenate([jnp.zeros((1,), jnp.int32), running]) + long_length


def locate(row_ids, bounds):
    passed = row_ids[:, None] >= bounds[None, :]
    segment = jnp.sum(passed.astype(jnp.int32), axis=1)
    seg_begin = jnp.max(jnp.where(passed, bounds[None, :], 0), axis=1)
    return (segment, seg_begin)


def rotate(parts, position, head_dim):
    half_dim = head_dim // 2
    inverse_freq = rope_base ** (-jnp.arange(half_dim, dtype=jnp.float32) / half_dim)
    angle = position[:, None, None] * inverse_freq[None, None, :]
    cosine = jnp.cos(angle)
    sine_part = jnp.sin(angle)
    first_half = parts[..., :half_dim]
    second_half = parts[..., half_dim:]
    return jnp.concatenate(
        [
            first_half * cosine - second_half * sine_part,
            second_half * cosine + first_half * sine_part,
        ],
        axis=-1,
    )


def body(stream_x, qkv_weight, short_lengths, cache_owner):
    seq_count = lax.axis_size("seq")
    tok_count = stream_x.shape[0]
    heads_here = qkv_weight.shape[1] // (3 * HD)
    long_length = tok_count * (seq_count * 11 // 16)
    bounds = boundaries(short_lengths, long_length)
    pad_segment = short_lengths.shape[0] + 1
    first_row = lax.axis_index("seq") * tok_count
    row_ids = first_row + jnp.arange(tok_count, dtype=jnp.int32)
    segment, seg_begin = locate(row_ids, bounds)
    position = (row_ids - seg_begin).astype(jnp.float32)
    is_padding = segment == pad_segment
    projected = jnp.dot(
        lax.all_gather(stream_x, "head", axis=1, tiled=True),
        qkv_weight,
        preferred_element_type=jnp.float32,
    )
    projected = projected.reshape(tok_count, heads_here, 3, HD)
    queries = rotate(projected[:, :, 0], position, HD).astype(jnp.bfloat16)
    rotated_keys = rotate(projected[:, :, 1], position, HD).astype(jnp.bfloat16)
    values = projected[:, :, 2].astype(jnp.bfloat16)
    packed = jnp.stack([rotated_keys, values], axis=2).reshape(tok_count, heads_here * 2 * HD)
    score_scale = 1.0 / math.sqrt(HD)
    shard_piece = lax.all_gather(packed, "seq", axis=0, tiled=True)
    key_count = shard_piece.shape[0]
    key_ids = jnp.arange(key_count, dtype=jnp.int32)
    row_max = jnp.full((heads_here, tok_count), neg_large, jnp.float32)
    key_segment, unused = locate(key_ids, bounds)
    key_value = shard_piece.reshape(key_count, heads_here, 2, HD)
    scores = (
        jnp.einsum("qhe,khe->hqk", queries, key_value[:, :, 0], preferred_element_type=jnp.float32)
        * score_scale
    )
    allowed = (
        (key_segment[None, :] == segment[:, None])
        & (key_ids[None, :] <= row_ids[:, None])
        & (key_ids[None, :] >= 0)
    )
    new_max = jnp.maximum(row_max, jnp.max(jnp.where(allowed[None], scores, neg_large), axis=2))
    weights = jnp.where(allowed[None], jnp.exp(scores - new_max[:, :, None]), 0.0)
    denominator = jnp.sum(weights, axis=2)
    context = jnp.einsum(
        "hqk,khe->hqe",
        weights.astype(jnp.bfloat16),
        key_value[:, :, 1],
        preferred_element_type=jnp.float32,
    )
    running = (new_max, denominator, context)
    row_max, denominator, context = running
    context = context / denominator[:, :, None]
    row_lse = jnp.where(is_padding[None, :], 0.0, row_max + jnp.log(denominator))
    context = jnp.where(is_padding[None, :, None], 0.0, context)
    attended = (
        jnp.transpose(context, (1, 0, 2)).reshape(tok_count, heads_here * HD).astype(jnp.bfloat16)
    )
    capacity = 2 * tok_count // seq_count
    owner_ids = cache_owner[:, 0]
    one_hot = (owner_ids[:, None] == jnp.arange(seq_count, dtype=jnp.int32)[None, :]).astype(
        jnp.int32
    )
    owner_rank = jnp.sum(jnp.cumsum(one_hot, axis=0) * one_hot, axis=1) - 1
    slot_index = owner_ids * capacity + owner_rank
    cached = jnp.where(is_padding[:, None], jnp.zeros_like(packed), packed)
    outbox = (
        jnp.zeros((seq_count * capacity, packed.shape[1]), jnp.bfloat16).at[slot_index].set(cached)
    )
    received = lax.all_to_all(
        outbox.reshape(seq_count, capacity, packed.shape[1]),
        "seq",
        split_axis=0,
        concat_axis=0,
        tiled=True,
    )
    kv_cache = received.reshape(seq_count * capacity, packed.shape[1])
    return (attended, row_lse, kv_cache)


def solution(mesh):
    return jax.shard_map(
        body,
        mesh=mesh,
        in_specs=(P("seq", "head"), P(None, "head"), P(), P("seq", None)),
        out_specs=(P("seq", "head"), P("head", "seq"), P("seq", "head")),
        check_vma=False,
    )
```

profile of v0, /device:TPU:6, one launch (start us, length us, event | category | flops | bytes accessed | tf_op | source)
XLA Modules:
  0.0 310.0 jit_solution(13779810520924512798)
XLA Ops:
  7.2 0.0 copy-start
  7.2 0.0 all-gather.3.cloned.1.call-start
  7.2 0.7 all-gather.3.cloned.1.call-update
  7.9 0.0 all-gather.5.cloned.1.call-start
  8.0 1.6 copy.28
  9.6 0.8 reduce-window.18
  10.3 0.6 reduce
  11.0 0.7 add_add_fusion
  11.7 0.0 copy-start.1
  11.7 0.1 fusion.29
  11.8 0.4 copy-done.1
  12.2 0.9 multiply_cosine_fusion
  13.1 32.1 %all-gather.3.cloned.1.call-done = bf16[256,3072]{1,0:T(8,128)(2,1)} async-done(((bf16[256,384]{1,0:T(8,128)(2,1)}), bf16[256,3072]{1,0:T(8,128)(2,1)}) %all-gather.3.cloned.1.call-update) | async-done | bytes 1572880 | tf_op jit(solution)/shard_map/all_gather | solution.py:57
  45.2 0.0 copy-done
  45.2 2.5 fusion.35
  47.8 1.5 subtract_convert_fusion.1
  49.3 0.7 copy.32
  50.0 0.0 all-gather.5.cloned.1.call-update
  50.0 1.3 fusion.26
  51.4 2.0 reduce-window.19
  53.3 1.0 slice_reduce_fusion
  54.4 1.0 fusion.25
  55.3 1.7 convert_reduce_fusion
  57.1 0.7 compare_select_fusion.1
  57.8 1.6 broadcast_select_fusion
  59.4 1.7 copy.36
  61.2 2.6 scatter_custom_fusion
  63.8 16.1 %all-to-all-start = ((bf16[64,8,384]{2,1,0:T(8,128)(2,1)}), bf16[64,8,384]{2,1,0:T(8,128)(2,1)}, u32[]{:S(2)}, u32[]{:S(2)}) async-start(bf16[64,8,384]{2,1,0:T(8,128)(2,1)} %bitcast.67), calls=%async_computation | async-start | bytes 786432 | tf_op jit(solution)/shard_map/all_to_all | solution.py:110
  79.8 8.0 %fusion.4 = pred[256,16384]{1,0:T(8,128)(4,1)} fusion(s32[256]{0:T(256)S(1)} %iota_add_fusion, s32[16384]{0:T(1024)} %convert_reduce_fusion, s32[256]{0:T(256)S(1)} %get-tuple-element.3), kind=kLoop, calls=%fused_computation.7 | loop fusion | flops 12582912 | bytes 4261888 | tf_op jit(solution)/shard_map/and | solution.py:78
  87.9 22.1 %all-to-all-done = bf16[64,8,384]{2,1,0:T(8,128)(2,1)} async-done(((bf16[64,8,384]{2,1,0:T(8,128)(2,1)}), bf16[64,8,384]{2,1,0:T(8,128)(2,1)}, u32[]{:S(2)}, u32[]{:S(2)}) %all-to-all-start) | async-done | bytes 393248 | tf_op jit(solution)/shard_map/all_to_all | solution.py:110
  109.9 140.7 %all-gather.5.cloned.1.call-done = bf16[16384,384]{0,1:T(8,128)(2,1)} async-done(((bf16[256,384]{0,1:T(8,128)(2,1)}), bf16[16384,384]{0,1:T(8,128)(2,1)}) %all-gather.5.cloned.1.call-update) | async-done | bytes 12582928 | tf_op jit(solution)/shard_map/all_gather | solution.py:67
  250.7 17.4 %select_reduce_fusion = (f32[2,256]{1,0:T(2,128)S(1)}, f32[2,256,16384]{2,1,0:T(8,128)}) fusion(pred[256,16384]{1,0:T(8,128)(4,1)} %fusion.4, bf16[16384,2,2,96]{0,3,2,1:T(8,128)(2,1)} %bitcast.76, bf16[256,2,48]{0,2,1:T(8,128)(2,1)} %get-tuple-element.8, bf16[256,2,48]{0,2,1:T(8,128)(2,1)} %get-tuple-element.7), kind=kOutput, calls=%fused_computation.2 | convolution fusion | flops 1635974656 | bytes 44140544 | tf_op jit(solution)/shard_map/qhe,khe->hqk/dot_general | solution.py:74
  268.0 15.9 %fusion = f32[2,256]{1,0:T(2,128)S(1)} fusion(f32[2,256,16384]{2,1,0:T(8,128)} %get-tuple-element.16, f32[2,256]{1,0:T(2,128)S(1)} %broadcast_maximum_fusion, pred[256,16384]{1,0:T(8,128)(4,1)} %fusion.4), kind=kLoop, calls=%fused_computation.3 | loop fusion | flops 33553920 | bytes 37752832 | tf_op jit(solution)/shard_map/reduce_sum | solution.py:84
  283.9 0.6 add_select_fusion
  284.5 16.9 %fusion.16 = bf16[256,2,96]{0,2,1:T(8,128)(2,1)} fusion(bf16[16384,2,2,96]{0,3,2,1:T(8,128)(2,1)} %bitcast.77, f32[2,256,16384]{2,1,0:T(8,128)} %get-tuple-element.16, f32[2,256]{1,0:T(2,128)S(1)} %broadcast_maximum_fusion, pred[256,16384]{1,0:T(8,128)(4,1)} %fusion.4, f32[256,2]{0,1:T(2,128)S(1)} %bitcast.72, pred[256]{0:T(512)(128)(4,1)S(1)} %broadcast_compare_fusion), kind=kOutput, calls=%fused_computation.17 | convolution fusion | flops 1644314624 | bytes 44142848 | tf_op jit(solution)/shard_map/hqk,khe->hqe/dot_general | solution.py:85
  301.4 1.8 copy.51
  (11 shorter events, 0.2 us)
Async XLA Ops:
  7.2 38.0 %copy-start = (bf16[3072,576]{0,1:T(8,128)(2,1)S(1)}, bf16[3072,576]{0,1:T(8,128)(2,1)}, u32[]{:S(2)}) copy-start(bf16[3072,576]{0,1:T(8,128)(2,1)} %param.5) | copy-start | bytes 10616836
  7.2 38.0 %all-gather.3.cloned.1.call-start = ((), (), s32[]{:S(2)}) async-start(), calls=%async_computation.1 | async-start | bytes 1769472 | tf_op jit(solution)/shard_map/all_gather | solution.py:57
  7.9 242.7 %all-gather.5.cloned.1.call-start = ((), (), s32[]{:S(2)}) async-start(), calls=%async_computation.2 | async-start | bytes 12779520 | tf_op jit(solution)/shard_map/all_gather | solution.py:67
  11.7 0.5 copy-start.1
  63.8 46.1 %all-to-all-start = ((bf16[64,8,384]{2,1,0:T(8,128)(2,1)}), bf16[64,8,384]{2,1,0:T(8,128)(2,1)}, u32[]{:S(2)}, u32[]{:S(2)}) async-start(bf16[64,8,384]{2,1,0:T(8,128)(2,1)} %bitcast.67), calls=%async_computation | async-start | bytes 786432 | tf_op jit(solution)/shard_map/all_to_all | solution.py:110
Sparse Core Ops, SparseCore 0:
  10.1 35.0 all-gather.2
  50.2 200.4 all-gather.4
where the time goes:
time: 312 us; the launch traced here: 310 us
  waiting for transfers between devices  196 us (63%)
  other arithmetic  37.5 us (12%)
  matrix products  36.8 us (12%)
  starting transfers between devices  16.1 us (5%)
  between operations  14.1 us (5%)
  local copies, waits for them, and re-layouts  9.93 us (3%)
    all_gather x1, waiting for transfers between devices, body(): shard_piece = lax.all_gather(packed, 'seq', axis=0, tiled=True)  141 us
    all_gather x1, waiting for transfers between devices, body(): lax.all_gather(stream_x, 'head', axis=1, tiled=True)  32.1 us
    all_to_all x1, waiting for transfers between devices, body(): lax.all_to_all(outbox.reshape(seq_count, capacity, packed.shape[1]), 'seq...  22.1 us
    dot_general x1, matrix products, body(): jnp.einsum('qhe,khe->hqk', queries, key_value[:, :, 0], preferred_element...  17.4 us
    dot_general x1, matrix products, body(): jnp.einsum('hqk,khe->hqe', weights.astype(jnp.bfloat16), key_value[:, :,...  16.9 us
    all_to_all x1, starting transfers between devices, body(): lax.all_to_all(outbox.reshape(seq_count, capacity, packed.shape[1]), 'seq...  16.1 us
    reduce_sum x1, other arithmetic, body(): denominator = jnp.sum(weights, axis=2)  15.9 us
    and x1, other arithmetic, body(): (key_segment[None, :] == segment[:, None]) & (key_ids[None, :] <= row_ids...  8.02 us
  transfers between devices with their start and end apart: 3, of which 3 were waited for; matrix products, arithmetic and copies ran while one was open for 9% of the time, Pallas kernels for 0%

commit v1 on v0

v1 whole, which is shorter than its diff:
```python
import functools
import math

import jax
import jax.numpy as jnp
from jax import lax
from jax.experimental import pallas as pl
from jax.experimental.pallas import tpu as pltpu
from jax.sharding import Mesh, PartitionSpec as P

HD = 96
CAP = 8
neg_large = -1e30
rope_base = 10000.0
score_scale = 1.0 / math.sqrt(HD)
log2_scale = score_scale * math.log2(math.e)


def boundaries(short_lengths, long_length):
    running = jnp.cumsum(short_lengths)
    return jnp.concatenate([jnp.zeros((1,), jnp.int32), running]) + long_length


def locate(row_ids, bounds):
    passed = row_ids[:, None] >= bounds[None, :]
    segment = jnp.sum(passed.astype(jnp.int32), axis=1)
    seg_begin = jnp.max(jnp.where(passed, bounds[None, :], 0), axis=1)
    return (segment, seg_begin)


def lane_ids(shape):
    return lax.broadcasted_iota(jnp.int32, shape, 1)


def half_projection(core_ref, x_ref, w_ref, out_ref):
    step = pl.program_id(0)
    part = jnp.dot(x_ref[0], w_ref[...], preferred_element_type=jnp.float32)

    @pl.when(step == 0)
    def _():
        out_ref[...] = part

    @pl.when(step > 0)
    def _():
        out_ref[...] += part


def pack_heads(p0, p1, p2, p3):
    lanes = lane_ids(p0.shape)
    r1 = pltpu.roll(p1, 96, 1)
    r2 = pltpu.roll(p2, 64, 1)
    r3 = pltpu.roll(p3, 32, 1)
    return (
        jnp.where(lanes < 96, p0, r1),
        jnp.where(lanes < 64, r1, r2),
        jnp.where(lanes < 32, r2, r3),
    )


def rest_projection(core_ref, x_ref, w_ref, first_ref, cos_ref, sin_ref, map_ref, q_ref, kv_ref, acc):
    step = pl.program_id(0)
    part = jnp.dot(x_ref[0], w_ref[...], preferred_element_type=jnp.float32)

    @pl.when(step == 0)
    def _():
        acc[:, :576] = first_ref[...] + part
        acc[:, 576:] = jnp.zeros_like(acc[:, 576:])

    @pl.when(step > 0)
    def _():
        acc[:, :576] += part

    @pl.when(step == pl.num_programs(0) - 1)
    def _():
        whole = acc[...]
        cosine = cos_ref[...]
        sine = sin_ref[...]
        lanes = lane_ids((whole.shape[0], 128))
        width = whole.shape[1]

        def window(first):
            return pltpu.roll(whole, (width - first) % width, 1)[:, :128]

        def rotated(first):
            here = window(first)
            ahead = window(first + 48)
            behind = window((first - 48) % width)
            return here * cosine + jnp.where(lanes < 48, ahead, behind) * sine

        def plain(first):
            return jnp.where(lanes < HD, window(first), 0.0)

        zero = jnp.zeros((whole.shape[0], 128), jnp.float32)
        queries = pack_heads(rotated(0), zero, rotated(288), zero)
        key_values = pack_heads(rotated(96), plain(192), rotated(384), plain(480))
        rows = q_ref.shape[0]
        for i in range(3):
            q_ref[:, 128 * i : 128 * i + 128] = queries[i].astype(jnp.bfloat16)
            kv_ref[:rows, 128 * i : 128 * i + 128] = key_values[i].astype(jnp.bfloat16)
        kv_ref[rows:, :] = jnp.broadcast_to(map_ref[...], (kv_ref.shape[0] - rows, 384)).astype(
            jnp.bfloat16
        )


def select_pages(table_ref, pages_ref, out_ref):
    targets, sources = out_ref.shape[:2]

    def one(i, carry):
        target = i % targets
        source = i // targets
        page = table_ref[i]
        rows = pages_ref[source, jnp.maximum(page, 0)]
        out_ref[target, source] = jnp.where(page >= 0, rows, jnp.zeros_like(rows))
        return carry

    lax.fori_loop(0, targets * sources, one, 0)


def attention(info_ref, q_ref, begin_ref, kv_ref, out_ref, scores):
    plane, column, low, masked_low = info_ref[0], info_ref[1], info_ref[2], info_ref[3]
    rows = q_ref.shape[0]
    keys = 256
    chunk = scores.shape[1]
    lanes = lane_ids((chunk, 128))

    for head in range(2):
        col = 0 if head == 0 else 128
        width = 128 if head == 0 else 256
        vcol = 0 if head == 0 else 256
        vwidth = 256 if head == 0 else 128
        for first in range(0, rows, chunk):
            q = q_ref[first : first + chunk, col : col + width]
            row_ids = plane * rows + first + lax.broadcasted_iota(jnp.int32, (chunk, keys), 0)

            def raw(j):
                k = kv_ref[j, :keys, col : col + width]
                return lax.dot_general(
                    q, k, (((1,), (1,)), ((), ())), preferred_element_type=jnp.float32
                )

            def fold(s):
                return jnp.maximum(s[:, :128], s[:, 128:])

            def free(j, top):
                s = raw(j)
                scores[j - low] = s
                return jnp.maximum(top, fold(s))

            def masked(j, top):
                key_ids = (
                    j * rows + column * keys + lax.broadcasted_iota(jnp.int32, (chunk, keys), 1)
                )
                begin = begin_ref[first : first + chunk, :]
                allowed = (key_ids <= row_ids) & (key_ids >= begin)
                s = jnp.where(allowed, raw(j), neg_large)
                scores[j - low] = s
                return jnp.maximum(top, fold(s))

            top = jnp.full((chunk, 128), neg_large, jnp.float32)
            top = lax.fori_loop(low, masked_low, free, top)
            top = lax.fori_loop(masked_low, plane + 1, masked, top)
            peak = jnp.max(top, axis=1, keepdims=True)

            def weigh(j, state):
                total, context = state
                p = jnp.exp2((scores[j - low] - peak) * log2_scale)
                v = kv_ref[j, :keys, vcol : vcol + vwidth]
                total = total + (p[:, :128] + p[:, 128:])
                context = context + jnp.dot(
                    p.astype(jnp.bfloat16), v, preferred_element_type=jnp.float32
                )
                return total, context

            total, context = lax.fori_loop(
                low,
                plane + 1,
                weigh,
                (
                    jnp.zeros((chunk, 128), jnp.float32),
                    jnp.zeros((chunk, vwidth), jnp.float32),
                ),
            )
            denominator = jnp.sum(total, axis=1, keepdims=True)
            if head == 0:
                left = pltpu.roll(context[:, :128], 32, 1)
                right = pltpu.roll(context[:, 128:], 32, 1)
                context = jnp.where(lanes < 32, left, right)
            else:
                context = pltpu.roll(context, 96, 1)
            context = context / denominator
            lse = peak * score_scale + jnp.log(denominator)
            coarse = lse.astype(jnp.bfloat16)
            rest = lse - coarse.astype(jnp.float32)
            middle = rest.astype(jnp.bfloat16)
            fine = rest - middle.astype(jnp.float32)
            packed = jnp.where(
                lanes < HD,
                context,
                jnp.where(
                    lanes == HD,
                    coarse.astype(jnp.float32),
                    jnp.where(lanes == HD + 1, middle.astype(jnp.float32), fine),
                ),
            )
            out_ref[first : first + chunk, head * 128 : head * 128 + 128] = packed.astype(
                jnp.bfloat16
            )


def combine(flag_ref, parts_ref, att_ref, lse_ref):
    count, rows = parts_ref.shape[:2]
    live = flag_ref[0] == 0
    heads = []
    for head in range(2):
        parts = [
            parts_ref[i, :, head * 128 : head * 128 + 128].astype(jnp.float32)
            for i in range(count)
        ]
        lses = [p[:, 96:97] + p[:, 97:98] + p[:, 98:99] for p in parts]
        peak = functools.reduce(jnp.maximum, lses)
        weights = [jnp.exp(v - peak) for v in lses]
        total = functools.reduce(jnp.add, weights)
        context = functools.reduce(jnp.add, [p * w for p, w in zip(parts, weights)])
        lanes = lane_ids(context.shape)
        context = jnp.where(live & (lanes < HD), context / total, 0.0)
        heads.append(context)
        lse = jnp.where(live, peak + jnp.log(total), 0.0)
        lse_ref[head : head + 1, :] = jnp.transpose(
            jnp.broadcast_to(lse, (rows, 128)), (1, 0)
        )[:1, :]
    lanes = lane_ids(heads[0].shape)
    moved = pltpu.roll(heads[1], 96, 1)
    att_ref[:, :128] = jnp.where(lanes < HD, heads[0], moved).astype(jnp.bfloat16)
    att_ref[:, 128:] = moved[:, :64].astype(jnp.bfloat16)


SMEM = pl.BlockSpec(memory_space=pltpu.SMEM)
VMEM = pl.BlockSpec(memory_space=pltpu.VMEM)


def project(core, gathered, weight, extra=None):
    blocks, rows, depth = gathered.shape
    columns = weight.shape[1]
    x_spec = pl.BlockSpec((1, rows, depth), lambda i, c: (i, 0, 0))
    w_spec = pl.BlockSpec((depth, columns), lambda i, c: (2 * i + c[0], 0))

    def fixed(shape):
        return pl.BlockSpec(shape, lambda i, c: (0,) * len(shape))

    if extra is None:
        return pl.pallas_call(
            half_projection,
            grid_spec=pltpu.PrefetchScalarGridSpec(
                num_scalar_prefetch=1,
                grid=(blocks,),
                in_specs=[x_spec, w_spec],
                out_specs=fixed((rows, columns)),
            ),
            out_shape=jax.ShapeDtypeStruct((rows, columns), jnp.float32),
        )(core, gathered, weight)
    first, cosine, sine, page_map = extra
    return pl.pallas_call(
        rest_projection,
        grid_spec=pltpu.PrefetchScalarGridSpec(
            num_scalar_prefetch=1,
            grid=(blocks,),
            in_specs=[
                x_spec,
                w_spec,
                fixed((rows, columns)),
                fixed((rows, 128)),
                fixed((rows, 128)),
                fixed((1, 384)),
            ],
            out_specs=[fixed((rows, 384)), fixed((rows + 16, 384))],
            scratch_shapes=[pltpu.VMEM((rows, 640), jnp.float32)],
        ),
        out_shape=[
            jax.ShapeDtypeStruct((rows, 384), jnp.bfloat16),
            jax.ShapeDtypeStruct((rows + 16, 384), jnp.bfloat16),
        ],
    )(core, gathered, weight, first, cosine, sine, page_map)


def body(stream_x, qkv_weight, short_lengths, cache_owner):
    planes, columns = lax.axis_size("z"), lax.axis_size("y")
    tok_count = stream_x.shape[0]
    plane, column = lax.axis_index("z"), lax.axis_index("y")
    core = lax.axis_index("c").astype(jnp.int32).reshape(1)
    plane_rows = tok_count * columns
    long_planes = planes * 11 // 16
    long_length = plane_rows * long_planes
    bounds = boundaries(short_lengths, long_length)
    pad_segment = short_lengths.shape[0] + 1

    ours = lax.all_gather(stream_x, "x", axis=0, tiled=False)
    theirs = lax.ppermute(ours, "c", [(0, 1), (1, 0)])

    first_row = plane * plane_rows + column * tok_count
    row_ids = first_row + jnp.arange(tok_count, dtype=jnp.int32)
    segment, seg_begin = locate(row_ids, bounds)
    position = (row_ids - seg_begin).astype(jnp.float32)
    half_dim = HD // 2
    inverse_freq = rope_base ** (-jnp.arange(half_dim, dtype=jnp.float32) / half_dim)
    angle = position[:, None] * inverse_freq[None, :]
    cosine = jnp.cos(angle)
    sine = jnp.sin(angle)
    blank = jnp.zeros((tok_count, 128 - HD), jnp.float32)
    cosine = jnp.concatenate([cosine, cosine, blank], axis=1)
    sine = jnp.concatenate([-sine, sine, blank], axis=1)

    pages = tok_count // CAP
    owners = planes * columns
    page_owner = cache_owner.reshape(pages, CAP)[:, 0]
    page_live = segment.reshape(pages, CAP)[:, 0] != pad_segment
    hit = (page_owner[:, None] == jnp.arange(owners, dtype=jnp.int32)[None, :]) & page_live[:, None]
    page_map = jnp.max(
        jnp.where(hit, jnp.arange(pages, dtype=jnp.int32)[:, None], -1), axis=0
    ).astype(jnp.float32)
    page_map = jnp.concatenate([page_map, jnp.zeros((384 - owners,), jnp.float32)])[None, :]

    half = project(core, ours, qkv_weight)
    queries, key_values = project(1 - core, theirs, qkv_weight, (half, cosine, sine, page_map))

    rows_sent = tok_count + 16
    gathered = lax.all_gather(key_values, "z", axis=0, tiled=True)
    plane_queries = lax.all_gather(queries, "y", axis=0, tiled=True)
    plane_ids = plane * plane_rows + jnp.arange(plane_rows, dtype=jnp.int32)
    unused, plane_begin = locate(plane_ids, bounds)

    is_long = plane < long_planes
    low = jnp.where(is_long, 0, jnp.maximum(plane - 1, long_planes))
    masked_low = jnp.where(is_long, plane, low)
    info = jnp.stack([plane, column, low, masked_low]).astype(jnp.int32)

    by_plane = gathered.reshape(planes, rows_sent, 384)
    table = lax.dynamic_slice_in_dim(
        by_plane[:, tok_count, :owners], plane * columns, columns, 1
    ).astype(jnp.int32)
    outbox = pl.pallas_call(
        select_pages,
        in_specs=[SMEM, VMEM],
        out_specs=VMEM,
        out_shape=jax.ShapeDtypeStruct((columns, planes, CAP, 384), jnp.bfloat16),
    )(table.reshape(-1), gathered.reshape(planes, rows_sent // CAP, CAP, 384))
    received = lax.all_to_all(
        outbox.reshape(columns, planes * CAP, 384), "y", split_axis=0, concat_axis=0, tiled=True
    )
    kv_cache = (
        received.reshape(columns, planes, CAP, 384)
        .transpose(1, 0, 2, 3)
        .reshape(planes * columns * CAP, 384)
    )

    chunk = 256
    partial = pl.pallas_call(
        attention,
        in_specs=[SMEM, VMEM, VMEM, VMEM],
        out_specs=VMEM,
        out_shape=jax.ShapeDtypeStruct((plane_rows, 256), jnp.bfloat16),
        scratch_shapes=[pltpu.VMEM((max(long_planes, 2), chunk, 256), jnp.float32)],
    )(info, plane_queries, plane_begin[:, None], by_plane)
    parts = lax.all_to_all(
        partial.reshape(columns, tok_count, 256), "y", split_axis=0, concat_axis=0, tiled=True
    )
    is_padding = (segment[:1] == pad_segment).astype(jnp.int32)
    attended, row_lse = pl.pallas_call(
        combine,
        in_specs=[SMEM, VMEM],
        out_specs=[VMEM, VMEM],
        out_shape=[
            jax.ShapeDtypeStruct((tok_count, 2 * HD), jnp.bfloat16),
            jax.ShapeDtypeStruct((2, tok_count), jnp.float32),
        ],
    )(is_padding, parts)
    return (attended, row_lse, kv_cache)


def solution(mesh):
    seq, head = mesh.devices.shape
    fine = Mesh(mesh.devices.reshape(seq // 4, 4, head // 2, 2), ("z", "y", "x", "c"))
    seq_axes, head_axes = ("z", "y"), ("x", "c")
    return jax.shard_map(
        body,
        mesh=fine,
        in_specs=(P(seq_axes, head_axes), P(None, head_axes), P(), P(seq_axes, None)),
        out_specs=(P(seq_axes, head_axes), P(head_axes, seq_axes), P(seq_axes, head_axes)),
        check_vma=False,
    )
```

time: 312 us -> 210 us (0.67)
  the two profiles are of different devices: /device:TPU:6 before, /device:TPU:320 now
where the time goes in v1:
time: 210 us; the launch traced here: 209 us
  waiting for transfers between devices  77.2 us (37%)
  Pallas kernels  58.9 us (28%)
  blocking collectives  29.8 us (14%)
  local copies, waits for them, and re-layouts  15.3 us (7%)
  between operations  14.8 us (7%)
  starting transfers between devices  9.7 us (5%)
  other arithmetic  3.49 us (2%)
    all_gather x1, waiting for transfers between devices, body(): gathered = lax.all_gather(key_values, 'z', axis=0, tiled=True)  71 us
    pallas_call x1, Pallas kernels, body(): pl.pallas_call(attention, in_specs=[SMEM, VMEM, VMEM, VMEM], out_specs=VM...  42.7 us
    all_gather x1, blocking collectives, body(): plane_queries = lax.all_gather(queries, 'y', axis=0, tiled=True)  15.9 us
    all_gather x1, blocking collectives, body(): ours = lax.all_gather(stream_x, 'x', axis=0, tiled=False)  13.9 us
    unnamed x13, local copies, waits for them, and re-layouts  9.93 us
    all_to_all x1, waiting for transfers between devices, body(): lax.all_to_all(partial.reshape(columns, tok_count, 256), 'y', split_axis=...  6.09 us
    pallas_call x1, Pallas kernels, project(): pl.pallas_call(rest_projection, grid_spec=pltpu.PrefetchScalarGridSpec(nu...  5.45 us
    pallas_call x1, Pallas kernels, project(): pl.pallas_call(half_projection, grid_spec=pltpu.PrefetchScalarGridSpec(nu...  4.37 us
  transfers between devices with their start and end apart: 4, of which 2 were waited for; matrix products, arithmetic and copies ran while one was open for 7% of the time, Pallas kernels for 22%

profile of v1, /device:TPU:320, one launch (start us, length us, event | category | flops | bytes accessed | tf_op | source)
XLA Modules:
  0.0 209.2 jit_solution(12454907921554410561)
XLA Ops:
  7.2 0.0 all-gather.3.cloned.1.call-start
  7.2 13.9 %all-gather = bf16[1024,384]{1,0:T(8,128)(2,1)S(1)} all-gather(bf16[256,384]{1,0:T(8,128)(2,1)} %param.4), channel_id=2, replica_groups=mesh['z'=16,'y'=4,'x'=4,'c'=2] {'x'}, dimensions={0}, use_global_device_ids=true | all-gather | bytes 983040 | tf_op jit(solution)/shard_map/all_gather | solution.py:296
  21.1 0.0 copy-start
  21.1 1.9 collective-permute-start
  23.0 0.7 copy.25
  23.8 0.1 reduce-window.8
  23.8 0.1 reduce
  23.9 6.1 %copy.27.w_ref = bf16[3072,576]{1,0:T(8,128)(2,1)} copy(bf16[3072,576]{0,1:T(8,128)(2,1)} %param.5) | data formatting | bytes 7077888 | tf_op args[1]
  30.0 0.0 copy-done
  30.0 0.0 copy-start.4
  30.0 4.4 %shard_map.67.first_ref = f32[256,576]{1,0:T(8,128)} custom-call(s32[1]{0:T(128)} %bitcast.5.core_ref, bf16[4,256,384]{2,1,0:T(8,128)(2,1)} %bitcast.21, bf16[3072,576]{1,0:T(8,128)(2,1)} %copy.27.w_ref), custom_call_target="tpu_custom_call" | custom-call | tf_op jit(solution)/shard_map/pallas_call | solution.py:251
  34.4 0.5 broadcast.39
  34.9 0.0 copy-done.4
  34.9 0.7 reduce.12
  35.6 0.1 reshape.101
  35.7 0.1 slice_reduce_fusion
  35.8 0.1 add_add_fusion
  35.9 0.1 fusion.2
  36.0 0.1 reshape.102
  36.1 0.1 fusion.4
  36.2 0.1 select_reduce_fusion.1
  36.3 0.6 broadcast_in_dim.57.map_ref
  36.9 0.1 pad.6.clone
  37.0 0.5 fusion
  37.5 0.9 maximum_maximum_fusion.1
  38.4 0.0 collective-permute-done.x_ref
  38.4 0.0 copy-start.2
  38.4 0.9 copy-done.2
  39.3 5.4 %shard_map.68 = (bf16[256,384]{1,0:T(8,128)(2,1)}, bf16[272,384]{1,0:T(8,128)(2,1)}) custom-call(s32[1]{0:T(128)S(6)} %sub.14.core_ref, bf16[4,256,384]{2,1,0:T(8,128)(2,1)} %copy-done.2, bf16[3072,576]{1,0:T(8,128)(2,1)} %copy.27.w_ref, f32[256,576]{1,0:T(8,128)} %shard_map.67.first_ref, f32[256,128]{1,0:T(8,128)} %get-tuple-element.29.cos_ref, ...), custom_call_target="tpu_custom_call" | custom-call | tf_op jit(solution)/shard_map/pallas_call | solution.py:262
  44.7 0.0 copy-start.3
  44.7 0.0 all-gather.3.cloned.1.call-update
  44.8 0.1 select_reduce_fusion
  44.9 1.0 copy.28.begin_ref
  45.9 0.6 pad_add_fusion.info_ref
  46.5 71.0 %all-gather.3.cloned.1.call-done = bf16[4352,384]{1,0:T(8,128)(2,1)} async-done(((bf16[272,384]{1,0:T(8,128)(2,1)}), bf16[4352,384]{1,0:T(8,128)(2,1)}) %all-gather.3.cloned.1.call-update) | async-done | bytes 3342352 | tf_op jit(solution)/shard_map/all_gather | solution.py:326
  117.6 0.8 slice.18
  118.3 0.1 convert_reduce_fusion
  118.4 0.6 reshape.109.table_ref
  119.0 3.7 %shard_map.71 = bf16[4,16,8,384]{3,2,1,0:T(8,128)(2,1)} custom-call(s32[64]{0:T(128)} %reshape.109.table_ref, bf16[16,34,8,384]{3,2,1,0:T(8,128)(2,1)} %bitcast.18), custom_call_target="tpu_custom_call" | custom-call | tf_op jit(solution)/shard_map/pallas_call | solution.py:340
  122.7 4.3 %all-to-all-start.1 = ((bf16[4,128,384]{2,1,0:T(8,128)(2,1)}), bf16[4,128,384]{2,1,0:T(8,128)(2,1)S(1)}, u32[]{:S(2)}, u32[]{:S(2)}) async-start(bf16[4,128,384]{2,1,0:T(8,128)(2,1)} %bitcast.24), calls=%async_computation.1 | async-start | bytes 786432 | tf_op jit(solution)/shard_map/all_to_all | solution.py:346
  127.0 0.0 copy-done.3
  127.0 15.9 %all_gather.14.q_ref = bf16[1024,384]{1,0:T(8,128)(2,1)} all-gather(bf16[256,384]{1,0:T(8,128)(2,1)S(1)} %copy-done.3), channel_id=1, replica_groups=mesh['z'=16,'y'=4,'x'=4,'c'=2] {'y'}, dimensions={0}, use_global_device_ids=true | all-gather | bytes 983040 | tf_op jit(solution)/shard_map/all_gather | solution.py:327
  142.9 42.7 %shard_map.69 = bf16[1024,256]{1,0:T(8,128)(2,1)} custom-call(s32[4]{0:T(128)} %pad_add_fusion.info_ref, bf16[1024,384]{1,0:T(8,128)(2,1)} %all_gather.14.q_ref, s32[1024,1]{1,0:T(8,128)} %copy.28.begin_ref, bf16[16,272,384]{2,1,0:T(8,128)(2,1)} %bitcast.19), custom_call_target="tpu_custom_call" | custom-call | tf_op jit(solution)/shard_map/pallas_call | solution.py:356
  185.6 0.0 all-to-all-done.1
  185.6 3.5 %all-to-all-start = ((bf16[4,256,256]{2,1,0:T(8,128)(2,1)}), bf16[4,256,256]{2,1,0:T(8,128)(2,1)S(1)}, u32[]{:S(2)}, u32[]{:S(2)}) async-start(bf16[4,256,256]{2,1,0:T(8,128)(2,1)} %bitcast.22), calls=%async_computation | async-start | bytes 1048576 | tf_op jit(solution)/shard_map/all_to_all | solution.py:363
  189.1 0.5 slice.12
  190.2 0.8 copy.29
  191.0 6.1 %all-to-all-done.parts_ref = bf16[4,256,256]{2,1,0:T(8,128)(2,1)S(1)} async-done(((bf16[4,256,256]{2,1,0:T(8,128)(2,1)}), bf16[4,256,256]{2,1,0:T(8,128)(2,1)S(1)}, u32[]{:S(2)}, u32[]{:S(2)}) %all-to-all-start) | async-done | bytes 524320 | tf_op jit(solution)/shard_map/all_to_all | solution.py:363
  197.1 0.0 copy-start.1
  197.1 0.8 copy-done.1
  197.9 2.8 %shard_map.70 = (bf16[256,192]{1,0:T(8,128)(2,1)}, f32[2,256]{1,0:T(2,128)}) custom-call(s32[1]{0:T(128)S(6)} %convert_element_type.24.flag_ref, bf16[4,256,256]{2,1,0:T(8,128)(2,1)} %copy-done.1), custom_call_target="tpu_custom_call" | custom-call | tf_op jit(solution)/shard_map/pallas_call | solution.py:367
  200.7 1.6 copy.30
  (7 shorter events, 0.0 us)
Async XLA Ops:
  7.2 110.4 %all-gather.3.cloned.1.call-start = ((), (), s32[]{:S(2)}) async-start(), calls=%async_computation.2 | async-start | bytes 3551232 | tf_op jit(solution)/shard_map/all_gather | solution.py:326
  21.1 9.0 %copy-start = (bf16[1024,384]{1,0:T(8,128)(2,1)}, bf16[1024,384]{1,0:T(8,128)(2,1)S(1)}, u32[]{:S(2)}) copy-start(bf16[1024,384]{1,0:T(8,128)(2,1)S(1)} %all-gather) | copy-start | bytes 2359300
  21.1 17.3 %collective-permute-start = (bf16[4,256,384]{2,1,0:T(8,128)(2,1)S(1)}, bf16[4,256,384]{2,1,0:T(8,128)(2,1)S(1)}, u32[]{:S(2)}, u32[]{:S(2)}) collective-permute-start(bf16[4,256,384]{2,1,0:T(8,128)(2,1)S(1)} %bitcast.20), channel_id=1, source_target_pairs={{0,1},{1,0},{2,3},{3,2},{4,5},{5,4},{6,7},{7,6},{8,9},{9,8},{10,11... | collective-permute-start | bytes 2359304 | tf_op jit(solution)/shard_map/ppermute | solution.py:297
  30.0 4.9 %copy-start.4 = (s32[256,1]{0,1:T(1,128)S(1)}, s32[256,1]{0,1:T(1,128)}, u32[]{:S(2)}) copy-start(s32[256,1]{0,1:T(1,128)} %param.7) | copy-start | bytes 3076
  38.4 0.9 copy-start.2
  44.7 82.3 %copy-start.3 = (bf16[256,384]{1,0:T(8,128)(2,1)S(1)}, bf16[256,384]{1,0:T(8,128)(2,1)}, u32[]{:S(2)}) copy-start(bf16[256,384]{1,0:T(8,128)(2,1)} %get-tuple-element.7) | copy-start | bytes 589828
  122.7 62.9 %all-to-all-start.1 = ((bf16[4,128,384]{2,1,0:T(8,128)(2,1)}), bf16[4,128,384]{2,1,0:T(8,128)(2,1)S(1)}, u32[]{:S(2)}, u32[]{:S(2)}) async-start(bf16[4,128,384]{2,1,0:T(8,128)(2,1)} %bitcast.24), calls=%async_computation.1 | async-start | bytes 786432 | tf_op jit(solution)/shard_map/all_to_all | solution.py:346
  185.6 11.5 %all-to-all-start = ((bf16[4,256,256]{2,1,0:T(8,128)(2,1)}), bf16[4,256,256]{2,1,0:T(8,128)(2,1)S(1)}, u32[]{:S(2)}, u32[]{:S(2)}) async-start(bf16[4,256,256]{2,1,0:T(8,128)(2,1)} %bitcast.22), calls=%async_computation | async-start | bytes 1048576 | tf_op jit(solution)/shard_map/all_to_all | solution.py:363
  197.1 0.8 copy-start.1
Sparse Core Ops, SparseCore 0:
  44.9 72.6 all-gather.2

commit v2 on v1

--- a/solution.py
+++ b/solution.py
@@ -34,7 +34,9 @@
 
 def half_projection(core_ref, x_ref, w_ref, out_ref):
     step = pl.program_id(0)
-    part = jnp.dot(x_ref[0], w_ref[...], preferred_element_type=jnp.float32)
+    part = lax.dot_general(
+        x_ref[...], w_ref[...], (((1,), (1,)), ((), ())), preferred_element_type=jnp.float32
+    )
 
     @pl.when(step == 0)
     def _():
@@ -59,7 +61,9 @@
 
 def rest_projection(core_ref, x_ref, w_ref, first_ref, cos_ref, sin_ref, map_ref, q_ref, kv_ref, acc):
     step = pl.program_id(0)
-    part = jnp.dot(x_ref[0], w_ref[...], preferred_element_type=jnp.float32)
+    part = lax.dot_general(
+        x_ref[...], w_ref[...], (((1,), (1,)), ((), ())), preferred_element_type=jnp.float32
+    )
 
     @pl.when(step == 0)
     def _():
@@ -116,101 +120,109 @@
     lax.fori_loop(0, targets * sources, one, 0)
 
 
-def attention(info_ref, q_ref, begin_ref, kv_ref, out_ref, scores):
+def attention(info_ref, q_ref, begin_ref, kv_ref, out_ref, scores, peaks, totals, contexts):
     plane, column, low, masked_low = info_ref[0], info_ref[1], info_ref[2], info_ref[3]
     rows = q_ref.shape[0]
     keys = 256
-    chunk = scores.shape[1]
+    chunk = 256
+    planes = kv_ref.shape[0]
+    count = plane + 1 - low
+    parts = [
+        (head, pl.ds(first, chunk), first) for head in range(2) for first in range(0, rows, chunk)
+    ]
+    key_cols = (slice(0, 128), slice(128, 384))
+    value_cols = (slice(0, 256), slice(256, 384))
+    value_width = (256, 128)
+
+    def score(j, masked):
+        for head, span, first in parts:
+            s = lax.dot_general(
+                q_ref[span, key_cols[head]],
+                kv_ref[j, :keys, key_cols[head]],
+                (((1,), (1,)), ((), ())),
+                preferred_element_type=jnp.float32,
+            )
+            if masked:
+                shape = (chunk, keys)
+                row_ids = plane * rows + first + lax.broadcasted_iota(jnp.int32, shape, 0)
+                key_ids = j * rows + column * keys + lax.broadcasted_iota(jnp.int32, shape, 1)
+                allowed = (key_ids <= row_ids) & (key_ids >= begin_ref[span, :])
+                s = jnp.where(allowed, s, neg_large)
+            scores[j - low, head, span, :] = s
+            peaks[head, span, :] = jnp.maximum(
+                peaks[head, span, :], jnp.maximum(s[:, :128], s[:, 128:])
+            )
+
+    peaks[...] = jnp.full_like(peaks, neg_large)
+    totals[...] = jnp.zeros_like(totals)
+    contexts[...] = jnp.zeros_like(contexts)
+
+    def free_step(j, carry):
+        score(j, False)
+        return carry
+
+    def masked_step(j, carry):
+        score(j, True)
+        return carry
+
+    lax.fori_loop(low, masked_low, free_step, 0)
+    lax.fori_loop(masked_low, plane + 1, masked_step, 0)
+
+    @pl.when(count % 2 == 1)
+    def _():
+        scores[count] = jnp.full(scores.shape[1:], neg_large, jnp.float32)
+
+    tops = []
+    for head, span, first in parts:
+        top = jnp.max(peaks[head, span, :], axis=1, keepdims=True)
+        tops.append(top)
+        peaks[head, span, :] = jnp.broadcast_to(top * log2_scale, (chunk, 128))
+
+    def weigh(i, carry):
+        for head, span, first in parts:
+            shift = peaks[head, span, :]
+            total = totals[head, span, :]
+            context = contexts[head, span, : value_width[head]]
+            for k in range(2):
+                slot = 2 * i + k
+                j = jnp.minimum(low + slot, planes - 1)
+                s = scores[slot, head, span, :]
+                left = jnp.exp2(s[:, :128] * log2_scale - shift)
+                right = jnp.exp2(s[:, 128:] * log2_scale - shift)
+                total = total + (left + right)
+                p = jnp.concatenate([left.astype(jnp.bfloat16), right.astype(jnp.bfloat16)], axis=1)
+                context = context + jnp.dot(
+                    p, kv_ref[j, :keys, value_cols[head]], preferred_element_type=jnp.float32
+                )
+            totals[head, span, :] = total
+            contexts[head, span, : value_width[head]] = context
+        return carry
+
+    lax.fori_loop(0, (count + 1) // 2, weigh, 0)
+
     lanes = lane_ids((chunk, 128))
-
-    for head in range(2):
-        col = 0 if head == 0 else 128
-        width = 128 if head == 0 else 256
-        vcol = 0 if head == 0 else 256
-        vwidth = 256 if head == 0 else 128
-        for first in range(0, rows, chunk):
-            q = q_ref[first : first + chunk, col : col + width]
-            row_ids = plane * rows + first + lax.broadcasted_iota(jnp.int32, (chunk, keys), 0)
-
-            def raw(j):
-                k = kv_ref[j, :keys, col : col + width]
-                return lax.dot_general(
-                    q, k, (((1,), (1,)), ((), ())), preferred_element_type=jnp.float32
-                )
-
-            def fold(s):
-                return jnp.maximum(s[:, :128], s[:, 128:])
-
-            def free(j, top):
-                s = raw(j)
-                scores[j - low] = s
-                return jnp.maximum(top, fold(s))
-
-            def masked(j, top):
-                key_ids = (
-                    j * rows + column * keys + lax.broadcasted_iota(jnp.int32, (chunk, keys), 1)
-                )
-                begin = begin_ref[first : first + chunk, :]
-                allowed = (key_ids <= row_ids) & (key_ids >= begin)
-                s = jnp.where(allowed, raw(j), neg_large)
-                scores[j - low] = s
-                return jnp.maximum(top, fold(s))
-
-            top = jnp.full((chunk, 128), neg_large, jnp.float32)
-            top = lax.fori_loop(low, masked_low, free, top)
-            top = lax.fori_loop(masked_low, plane + 1, masked, top)
-            peak = jnp.max(top, axis=1, keepdims=True)
-
-            def weigh(j, state):
-                total, context = state
-                p = jnp.exp2((scores[j - low] - peak) * log2_scale)
-                v = kv_ref[j, :keys, vcol : vcol + vwidth]
-                total = total + (p[:, :128] + p[:, 128:])
-                context = context + jnp.dot(
-                    p.astype(jnp.bfloat16), v, preferred_element_type=jnp.float32
-                )
-                return total, context
-
-            total, context = lax.fori_loop(
-                low,
-                plane + 1,
-                weigh,
-                (
-                    jnp.zeros((chunk, 128), jnp.float32),
-                    jnp.zeros((chunk, vwidth), jnp.float32),
-                ),
-            )
-            denominator = jnp.sum(total, axis=1, keepdims=True)
-            if head == 0:
-                left = pltpu.roll(context[:, :128], 32, 1)
-                right = pltpu.roll(context[:, 128:], 32, 1)
-                context = jnp.where(lanes < 32, left, right)
-            else:
-                context = pltpu.roll(context, 96, 1)
-            context = context / denominator
-            lse = peak * score_scale + jnp.log(denominator)
-            coarse = lse.astype(jnp.bfloat16)
-            rest = lse - coarse.astype(jnp.float32)
-            middle = rest.astype(jnp.bfloat16)
-            fine = rest - middle.astype(jnp.float32)
-            packed = jnp.where(
-                lanes < HD,
-                context,
-                jnp.where(
-                    lanes == HD,
-                    coarse.astype(jnp.float32),
-                    jnp.where(lanes == HD + 1, middle.astype(jnp.float32), fine),
-                ),
-            )
-            out_ref[first : first + chunk, head * 128 : head * 128 + 128] = packed.astype(
-                jnp.bfloat16
-            )
+    for (head, span, first), top in zip(parts, tops):
+        denominator = jnp.sum(totals[head, span, :], axis=1, keepdims=True)
+        if head == 0:
+            left = pltpu.roll(contexts[head, span, :128], 32, 1)
+            right = pltpu.roll(contexts[head, span, 128:], 32, 1)
+            context = jnp.where(lanes < 32, left, right)
+        else:
+            context = pltpu.roll(contexts[head, span, :128], 96, 1)
+        context = context / denominator
+        lse = top * score_scale + jnp.log(denominator)
+        coarse = lse.astype(jnp.bfloat16).astype(jnp.float32)
+        middle = (lse - coarse).astype(jnp.bfloat16).astype(jnp.float32)
+        fine = lse - coarse - middle
+        tail = jnp.where(lanes == HD, coarse, jnp.where(lanes == HD + 1, middle, fine))
+        out_ref[span, head * 128 : head * 128 + 128] = jnp.where(
+            lanes < HD, context, tail
+        ).astype(jnp.bfloat16)
 
 
 def combine(flag_ref, parts_ref, att_ref, lse_ref):
-    count, rows = parts_ref.shape[:2]
+    count = parts_ref.shape[0]
     live = flag_ref[0] == 0
-    heads = []
     for head in range(2):
         parts = [
             parts_ref[i, :, head * 128 : head * 128 + 128].astype(jnp.float32)
@@ -222,16 +234,10 @@
         total = functools.reduce(jnp.add, weights)
         context = functools.reduce(jnp.add, [p * w for p, w in zip(parts, weights)])
         lanes = lane_ids(context.shape)
-        context = jnp.where(live & (lanes < HD), context / total, 0.0)
-        heads.append(context)
-        lse = jnp.where(live, peak + jnp.log(total), 0.0)
-        lse_ref[head : head + 1, :] = jnp.transpose(
-            jnp.broadcast_to(lse, (rows, 128)), (1, 0)
-        )[:1, :]
-    lanes = lane_ids(heads[0].shape)
-    moved = pltpu.roll(heads[1], 96, 1)
-    att_ref[:, :128] = jnp.where(lanes < HD, heads[0], moved).astype(jnp.bfloat16)
-    att_ref[:, 128:] = moved[:, :64].astype(jnp.bfloat16)
+        whole = jnp.where(lanes < HD, context / total, peak + jnp.log(total))
+        turned = jnp.where(live, jnp.transpose(whole, (1, 0)), 0.0)
+        att_ref[head * HD : head * HD + HD, :] = turned[:HD].astype(jnp.bfloat16)
+        lse_ref[head : head + 1, :] = turned[HD : HD + 1]
 
 
 SMEM = pl.BlockSpec(memory_space=pltpu.SMEM)
@@ -239,10 +245,12 @@
 
 
 def project(core, gathered, weight, extra=None):
-    blocks, rows, depth = gathered.shape
-    columns = weight.shape[1]
-    x_spec = pl.BlockSpec((1, rows, depth), lambda i, c: (i, 0, 0))
-    w_spec = pl.BlockSpec((depth, columns), lambda i, c: (2 * i + c[0], 0))
+    depth = gathered.shape[1]
+    columns = weight.shape[0]
+    blocks = weight.shape[1] // (2 * depth)
+    rows = gathered.shape[0] // blocks
+    x_spec = pl.BlockSpec((rows, depth), lambda i, c: (i, 0))
+    w_spec = pl.BlockSpec((columns, depth), lambda i, c: (0, 2 * i + c[0]))
 
     def fixed(shape):
         return pl.BlockSpec(shape, lambda i, c: (0,) * len(shape))
@@ -293,7 +301,7 @@
     bounds = boundaries(short_lengths, long_length)
     pad_segment = short_lengths.shape[0] + 1
 
-    ours = lax.all_gather(stream_x, "x", axis=0, tiled=False)
+    ours = lax.all_gather(stream_x, "x", axis=0, tiled=True)
     theirs = lax.ppermute(ours, "c", [(0, 1), (1, 0)])
 
     first_row = plane * plane_rows + column * tok_count
@@ -319,8 +327,9 @@
     ).astype(jnp.float32)
     page_map = jnp.concatenate([page_map, jnp.zeros((384 - owners,), jnp.float32)])[None, :]
 
-    half = project(core, ours, qkv_weight)
-    queries, key_values = project(1 - core, theirs, qkv_weight, (half, cosine, sine, page_map))
+    weight = qkv_weight.T
+    half = project(core, ours, weight)
+    queries, key_values = project(1 - core, theirs, weight, (half, cosine, sine, page_map))
 
     rows_sent = tok_count + 16
     gathered = lax.all_gather(key_values, "z", axis=0, tiled=True)
@@ -332,6 +341,11 @@
     low = jnp.where(is_long, 0, jnp.maximum(plane - 1, long_planes))
     masked_low = jnp.where(is_long, plane, low)
     info = jnp.stack([plane, column, low, masked_low]).astype(jnp.int32)
+
+    plane_begin = plane_begin[:, None]
+    gathered, plane_queries, plane_begin, info = lax.optimization_barrier(
+        (gathered, plane_queries, plane_begin, info)
+    )
 
     by_plane = gathered.reshape(planes, rows_sent, 384)
     table = lax.dynamic_slice_in_dim(
@@ -352,14 +366,19 @@
         .reshape(planes * columns * CAP, 384)
     )
 
-    chunk = 256
+    slots = 2 * ((max(long_planes, 2) + 1) // 2)
     partial = pl.pallas_call(
         attention,
         in_specs=[SMEM, VMEM, VMEM, VMEM],
         out_specs=VMEM,
         out_shape=jax.ShapeDtypeStruct((plane_rows, 256), jnp.bfloat16),
-        scratch_shapes=[pltpu.VMEM((max(long_planes, 2), chunk, 256), jnp.float32)],
-    )(info, plane_queries, plane_begin[:, None], by_plane)
+        scratch_shapes=[
+            pltpu.VMEM((slots, 2, plane_rows, 256), jnp.float32),
+            pltpu.VMEM((2, plane_rows, 128), jnp.float32),
+            pltpu.VMEM((2, plane_rows, 128), jnp.float32),
+            pltpu.VMEM((2, plane_rows, 256), jnp.float32),
+        ],
+    )(info, plane_queries, plane_begin, by_plane)
     parts = lax.all_to_all(
         partial.reshape(columns, tok_count, 256), "y", split_axis=0, concat_axis=0, tiled=True
     )
@@ -369,11 +388,11 @@
         in_specs=[SMEM, VMEM],
         out_specs=[VMEM, VMEM],
         out_shape=[
-            jax.ShapeDtypeStruct((tok_count, 2 * HD), jnp.bfloat16),
+            jax.ShapeDtypeStruct((2 * HD, tok_count), jnp.bfloat16),
             jax.ShapeDtypeStruct((2, tok_count), jnp.float32),
         ],
     )(is_padding, parts)
-    return (attended, row_lse, kv_cache)
+    return (attended.T, row_lse, kv_cache)
 
 
 def solution(mesh):

time: 210 us -> 161 us (0.77)
  the two profiles are of different devices: /device:TPU:320 before, /device:TPU:6 now
where the time goes in v2:
time: 161 us; the launch traced here: 160 us
  waiting for transfers between devices  70.1 us (44%)
  blocking collectives  31 us (19%)
  Pallas kernels  22.7 us (14%)
  between operations  14.8 us (9%)
  starting transfers between devices  10.1 us (6%)
  local copies, waits for them, and re-layouts  7.53 us (5%)
  other arithmetic  3.46 us (2%)
    all_gather x1, waiting for transfers between devices, body(): gathered = lax.all_gather(key_values, 'z', axis=0, tiled=True)  63 us
    all_gather x1, blocking collectives, body(): ours = lax.all_gather(stream_x, 'x', axis=0, tiled=True)  16.2 us
    all_gather x1, blocking collectives, body(): plane_queries = lax.all_gather(queries, 'y', axis=0, tiled=True)  14.8 us
    pallas_call x1, Pallas kernels, body(): pl.pallas_call(attention, in_specs=[SMEM, VMEM, VMEM, VMEM], out_specs=VM...  6.31 us
    all_to_all x1, waiting for transfers between devices, body(): lax.all_to_all(partial.reshape(columns, tok_count, 256), 'y', split_axis=...  6.13 us
    pallas_call x1, Pallas kernels, project(): pl.pallas_call(rest_projection, grid_spec=pltpu.PrefetchScalarGridSpec(nu...  5.53 us
    pallas_call x1, Pallas kernels, project(): pl.pallas_call(half_projection, grid_spec=pltpu.PrefetchScalarGridSpec(nu...  4.44 us
    all_to_all x1, starting transfers between devices, body(): lax.all_to_all(outbox.reshape(columns, planes * CAP, 384), 'y', split_axi...  4.24 us
  transfers between devices with their start and end apart: 4, of which 3 were waited for; matrix products, arithmetic and copies ran while one was open for 5% of the time, Pallas kernels for 7%

profile of v2, /device:TPU:6, one launch (start us, length us, event | category | flops | bytes accessed | tf_op | source)
XLA Modules:
  0.0 159.7 jit_solution(4857957439482775303)
XLA Ops:
  7.2 0.0 copy-start.3
  7.2 0.0 all-gather.2.cloned.1.call-start
  7.2 16.2 %all_gather.9.x_ref = bf16[1024,384]{1,0:T(8,128)(2,1)S(1)} all-gather(bf16[256,384]{1,0:T(8,128)(2,1)} %param.4), channel_id=1, replica_groups=mesh['z'=16,'y'=4,'x'=4,'c'=2] {'x'}, dimensions={0}, use_global_device_ids=true | all-gather | bytes 983040 | tf_op jit(solution)/shard_map/all_gather | solution.py:304
  23.4 0.0 copy-start
  23.4 1.9 %collective-permute-start = (bf16[1024,384]{1,0:T(8,128)(2,1)S(1)}, bf16[1024,384]{1,0:T(8,128)(2,1)S(1)}, u32[]{:S(2)}, u32[]{:S(2)}) collective-permute-start(bf16[1024,384]{1,0:T(8,128)(2,1)S(1)} %all_gather.9.x_ref), channel_id=1, source_target_pairs={{0,1},{1,0},{2,3},{3,2},{4,5},{5,4},{6,7},{7,6},{8,9},{9,8},{10,11... | collective-permute-start | bytes 2359304 | tf_op jit(solution)/shard_map/ppermute | solution.py:305
  25.3 0.7 copy.16
  26.1 0.1 reduce-window.8
  26.1 0.1 reduce
  26.3 0.0 copy-done
  26.3 4.4 %shard_map.67.first_ref = f32[256,576]{1,0:T(8,128)} custom-call(s32[1]{0:T(128)} %bitcast.1.core_ref, bf16[1024,384]{1,0:T(8,128)(2,1)} %copy-done, bf16[576,3072]{1,0:T(8,128)(2,1)} %bitcast.18), custom_call_target="tpu_custom_call" | custom-call | tf_op jit(solution)/shard_map/pallas_call | solution.py:259
  30.7 0.5 broadcast.39
  31.2 0.0 copy-done.3
  31.2 0.7 reduce.12
  31.9 0.1 reshape.101
  32.0 0.1 slice_reduce_fusion
  32.1 0.1 add_add_fusion
  32.2 0.1 fusion.2
  32.3 0.1 reshape.102
  32.3 0.1 fusion.4
  32.5 0.1 select_reduce_fusion.1
  32.6 0.6 broadcast_in_dim.57.map_ref
  33.2 0.1 pad.10.clone
  33.3 0.5 fusion
  33.8 0.8 maximum_maximum_fusion.1
  34.6 0.0 collective-permute-done.x_ref
  34.7 0.0 copy-start.2
  34.7 0.9 copy-done.2
  35.5 5.5 %shard_map.68 = (bf16[256,384]{1,0:T(8,128)(2,1)}, bf16[272,384]{1,0:T(8,128)(2,1)}) custom-call(s32[1]{0:T(128)S(6)} %sub.13.core_ref, bf16[1024,384]{1,0:T(8,128)(2,1)} %copy-done.2, bf16[576,3072]{1,0:T(8,128)(2,1)} %bitcast.19, f32[256,576]{1,0:T(8,128)} %shard_map.67.first_ref, f32[256,128]{1,0:T(8,128)} %get-tuple-element.25.cos_ref, ...), custom_call_target="tpu_custom_call" | custom-call | tf_op jit(solution)/shard_map/pallas_call | solution.py:270
  41.1 0.0 all-gather.2.cloned.1.call-update
  41.1 0.6 pad_add_fusion.info_ref
  41.7 0.1 select_reduce_fusion
  41.8 14.8 %all_gather.11.q_ref = bf16[1024,384]{1,0:T(8,128)(2,1)} all-gather(bf16[256,384]{1,0:T(8,128)(2,1)} %get-tuple-element.12), channel_id=1, replica_groups=mesh['z'=16,'y'=4,'x'=4,'c'=2] {'y'}, dimensions={0}, use_global_device_ids=true | all-gather | bytes 983040 | tf_op jit(solution)/shard_map/all_gather | solution.py:336
  56.7 63.0 %all-gather.2.cloned.1.call-done = bf16[4352,384]{1,0:T(8,128)(2,1)} async-done(((bf16[272,384]{1,0:T(8,128)(2,1)}), bf16[4352,384]{1,0:T(8,128)(2,1)}) %all-gather.2.cloned.1.call-update) | async-done | bytes 3342352 | tf_op jit(solution)/shard_map/all_gather | solution.py:335
  119.7 0.8 slice.18
  120.4 0.1 convert_reduce_fusion
  120.5 0.6 reshape.109.table_ref
  121.1 3.7 %shard_map.71 = bf16[4,16,8,384]{3,2,1,0:T(8,128)(2,1)} custom-call(s32[64]{0:T(128)} %reshape.109.table_ref, bf16[16,34,8,384]{3,2,1,0:T(8,128)(2,1)} %bitcast.21), custom_call_target="tpu_custom_call" | custom-call | tf_op jit(solution)/shard_map/pallas_call | solution.py:354
  124.8 4.2 %all-to-all-start.1 = ((bf16[4,128,384]{2,1,0:T(8,128)(2,1)}), bf16[4,128,384]{2,1,0:T(8,128)(2,1)S(1)}, u32[]{:S(2)}, u32[]{:S(2)}) async-start(bf16[4,128,384]{2,1,0:T(8,128)(2,1)} %bitcast.25), calls=%async_computation.1 | async-start | bytes 786432 | tf_op jit(solution)/shard_map/all_to_all | solution.py:360
  129.1 1.0 copy.17.begin_ref
  130.1 6.3 %shard_map.69 = bf16[1024,256]{1,0:T(8,128)(2,1)} custom-call(s32[4]{0:T(128)} %pad_add_fusion.info_ref, bf16[1024,384]{1,0:T(8,128)(2,1)} %all_gather.11.q_ref, s32[1024,1]{1,0:T(8,128)} %copy.17.begin_ref, bf16[16,272,384]{2,1,0:T(8,128)(2,1)} %bitcast.22), custom_call_target="tpu_custom_call" | custom-call | tf_op jit(solution)/shard_map/pallas_call | solution.py:370
  136.4 0.9 all-to-all-done.1
  137.3 3.9 %all-to-all-start = ((bf16[4,256,256]{2,1,0:T(8,128)(2,1)}), bf16[4,256,256]{2,1,0:T(8,128)(2,1)S(1)}, u32[]{:S(2)}, u32[]{:S(2)}) async-start(bf16[4,256,256]{2,1,0:T(8,128)(2,1)} %bitcast.23), calls=%async_computation | async-start | bytes 1048576 | tf_op jit(solution)/shard_map/all_to_all | solution.py:382
  141.2 0.5 slice.12
  142.4 0.8 copy.18
  143.2 6.1 %all-to-all-done.parts_ref = bf16[4,256,256]{2,1,0:T(8,128)(2,1)S(1)} async-done(((bf16[4,256,256]{2,1,0:T(8,128)(2,1)}), bf16[4,256,256]{2,1,0:T(8,128)(2,1)S(1)}, u32[]{:S(2)}, u32[]{:S(2)}) %all-to-all-start) | async-done | bytes 524320 | tf_op jit(solution)/shard_map/all_to_all | solution.py:382
  149.3 0.0 copy-start.1
  149.3 0.8 copy-done.1
  150.1 2.7 %shard_map.70 = (bf16[192,256]{1,0:T(8,128)(2,1)}, f32[2,256]{1,0:T(2,128)}) custom-call(s32[1]{0:T(128)S(6)} %convert_element_type.24.flag_ref, bf16[4,256,256]{2,1,0:T(8,128)(2,1)} %copy-done.1), custom_call_target="tpu_custom_call" | custom-call | tf_op jit(solution)/shard_map/pallas_call | solution.py:386
  (7 shorter events, 0.0 us)
Async XLA Ops:
  7.2 24.1 %copy-start.3 = (s32[256,1]{0,1:T(1,128)S(1)}, s32[256,1]{0,1:T(1,128)}, u32[]{:S(2)}) copy-start(s32[256,1]{0,1:T(1,128)} %param.7) | copy-start | bytes 3076
  7.2 112.5 %all-gather.2.cloned.1.call-start = ((), (), s32[]{:S(2)}) async-start(), calls=%async_computation.2 | async-start | bytes 3551232 | tf_op jit(solution)/shard_map/all_gather | solution.py:335
  23.4 2.9 %copy-start = (bf16[1024,384]{1,0:T(8,128)(2,1)}, bf16[1024,384]{1,0:T(8,128)(2,1)S(1)}, u32[]{:S(2)}) copy-start(bf16[1024,384]{1,0:T(8,128)(2,1)S(1)} %all_gather.9.x_ref) | copy-start | bytes 2359300
  23.4 11.2 %collective-permute-start = (bf16[1024,384]{1,0:T(8,128)(2,1)S(1)}, bf16[1024,384]{1,0:T(8,128)(2,1)S(1)}, u32[]{:S(2)}, u32[]{:S(2)}) collective-permute-start(bf16[1024,384]{1,0:T(8,128)(2,1)S(1)} %all_gather.9.x_ref), channel_id=1, source_target_pairs={{0,1},{1,0},{2,3},{3,2},{4,5},{5,4},{6,7},{7,6},{8,9},{9,8},{10,11... | collective-permute-start | bytes 2359304 | tf_op jit(solution)/shard_map/ppermute | solution.py:305
  34.7 0.9 copy-start.2
  124.8 12.5 %all-to-all-start.1 = ((bf16[4,128,384]{2,1,0:T(8,128)(2,1)}), bf16[4,128,384]{2,1,0:T(8,128)(2,1)S(1)}, u32[]{:S(2)}, u32[]{:S(2)}) async-start(bf16[4,128,384]{2,1,0:T(8,128)(2,1)} %bitcast.25), calls=%async_computation.1 | async-start | bytes 786432 | tf_op jit(solution)/shard_map/all_to_all | solution.py:360
  137.3 12.0 %all-to-all-start = ((bf16[4,256,256]{2,1,0:T(8,128)(2,1)}), bf16[4,256,256]{2,1,0:T(8,128)(2,1)S(1)}, u32[]{:S(2)}, u32[]{:S(2)}) async-start(bf16[4,256,256]{2,1,0:T(8,128)(2,1)} %bitcast.23), calls=%async_computation | async-start | bytes 1048576 | tf_op jit(solution)/shard_map/all_to_all | solution.py:382
  149.3 0.8 copy-start.1
Sparse Core Ops, SparseCore 0:
  41.2 78.4 all-gather.1
